TPU v7x, 32 devices: a whole 2x2x4 slice. The times are simulated.
32 devices in a mesh: feat: 4 (over z), tok: 8 (over y, x, core).
Axes of the slice: x: 2, y: 2, z: 4, core: 2. Of those that a mesh axis runs over, the one named last changes fastest.
Arguments:
- tokens: bfloat16 [512, 8192], P('tok'), may hold values from -6 to 6
- dec_bias: bfloat16 [8192], replicated, may hold values from -3 to 3
- enc_weight: bfloat16 [8192, 8192], P('tok', 'feat'), may hold values from -0.0625 to 0.0625
- enc_bias: bfloat16 [8192], P('feat'), may hold values from -3 to 3
- dec_weight: bfloat16 [8192, 8192], P('feat', 'tok'), may hold values from -0.25 to 0.25
- block_ids: int32 [8, 4, 4], P(None, 'feat'), may hold values from 0 to 31, as said below
- block_counts: int32 [8, 4], P(None, 'feat'), may hold values from 1 to 4, as said below
Outputs:
- code_values: bfloat16 [512, 1024], P('tok', 'feat')
- rebuilt: bfloat16 [512, 8192], P('tok', 'feat')
Inputs may be any that keep to these rules, and one draw needn't show every extreme that they name: `block_ids`: the 4 entries of one list are distinct; they number the owner's 32 blocks. `block_counts`: for every owner some tile has all 4 slots active.
All inputs are finite; a program needn't handle non-finite values.
Results may differ from a plain program's by a relative error of at most 0.029.
Values may be sent and summed in bfloat16 or wider, within the bound.
No kernel may reach another device: no remote copies, remote signals or barrier semaphores. Data moves between devices by JAX's collectives and lax.ppermute only.
A program may use at most 64 MiB of HBM per device.

v0:
```python
import jax
import jax.numpy as jnp
from jax import lax
from jax.sharding import PartitionSpec as P

BLOCK = 64
SLOTS = 4


def on_device(tokens, dec_bias, enc_weight, enc_bias, dec_weight, block_ids, block_counts):
    tile_count = lax.axis_size("tok")
    tok_rows = tokens.shape[0]
    width = tokens.shape[1]
    wslice = width // tile_count
    nblocks = enc_weight.shape[1] // BLOCK
    active_cols = SLOTS * BLOCK
    listed = block_ids[:, 0, :].reshape(-1)
    centered = (tokens.astype(jnp.float32) - dec_bias.astype(jnp.float32)).astype(jnp.bfloat16)
    chosen = jnp.take(enc_weight.reshape(wslice, nblocks, BLOCK), listed, axis=1)
    chosen = chosen.reshape(wslice, tile_count, active_cols)
    gathered = lax.all_to_all(centered, "tok", split_axis=1, concat_axis=0, tiled=True)
    gathered = gathered.reshape(tile_count, tok_rows, wslice)
    pre = lax.psum_scatter(
        jnp.einsum("tri,itc->trc", gathered, chosen, preferred_element_type=jnp.float32).astype(
            jnp.bfloat16
        ),
        "tok",
        scatter_dimension=0,
        tiled=True,
    ).astype(jnp.float32)[0]
    my_tile = lax.axis_index("tok")
    my_ids = lax.dynamic_slice_in_dim(block_ids[:, 0, :], my_tile, 1, 0)[0]
    my_count = lax.dynamic_slice_in_dim(block_counts[:, 0], my_tile, 1, 0)[0]
    bias_cols = jnp.take(enc_bias.reshape(nblocks, BLOCK), my_ids, axis=0).reshape(active_cols)
    live_mask = jnp.repeat(jnp.arange(SLOTS, dtype=jnp.int32) < my_count, BLOCK)
    code_values = jnp.where(
        live_mask[None, :], jnp.maximum(pre + bias_cols.astype(jnp.float32)[None, :], 0.0), 0.0
    )
    code_values = code_values.astype(jnp.bfloat16)
    outgoing = jnp.take(dec_weight.reshape(nblocks, BLOCK, wslice), listed, axis=0)
    outgoing = outgoing.reshape(tile_count, active_cols, wslice)
    owner_part = jnp.einsum(
        "rc,uci->rui",
        code_values,
        lax.all_to_all(outgoing, "tok", split_axis=0, concat_axis=0, tiled=True),
        preferred_element_type=jnp.float32,
    )
    owner_part = owner_part.reshape(tok_rows, width)
    summed = lax.psum_scatter(
        owner_part.astype(jnp.bfloat16), "feat", scatter_dimension=1, tiled=True
    ).astype(jnp.float32)
    share = summed.shape[1]
    bias_share = lax.dynamic_slice_in_dim(dec_bias, lax.axis_index("feat") * share, share, 0)
    rebuilt = (summed + bias_share.astype(jnp.float32)[None, :]).astype(jnp.bfloat16)
    return (code_values, rebuilt)


def solution(mesh):
    in_specs = (
        P("tok", None),
        P(),
        P("tok", "feat"),
        P("feat"),
        P("feat", "tok"),
        P(None, "feat", None),
        P(None, "feat"),
    )
    out_specs = (P("tok", "feat"), P("tok", "feat"))
    return jax.shard_map(
        on_device, mesh=mesh, in_specs=in_specs, out_specs=out_specs, check_vma=False
    )
```

profile of v0, /device:TPU:0, one launch (start us, length us, event | category | flops | bytes accessed | tf_op | source)
XLA Modules:
  0.0 131.7 jit_solution(5689210240074162982)
XLA Ops:
  7.2 0.0 copy-start
  7.2 0.0 copy-start.2
  7.2 0.7 convert_element_type.46
  7.9 1.4 %subtract_convert_fusion = bf16[64,8192]{1,0:T(8,128)(2,1)S(1)} fusion(bf16[64,8192]{1,0:T(8,128)(2,1)} %param.7, f32[8192]{0:T(1024)S(1)} %convert_element_type.46), kind=kLoop, calls=%fused_computation.9 | loop fusion | flops 1572864 | bytes 2129920 | tf_op jit(solution)/shard_map/convert_element_type | solution.py:18
  9.3 1.1 copy.25
  10.4 5.2 %all-to-all-start = ((bf16[64,8,1024]{2,0,1:T(8,128)(2,1)}), bf16[64,8,1024]{2,0,1:T(8,128)(2,1)S(1)}, u32[]{:S(2)}, u32[]{:S(2)}) async-start(bf16[64,8,1024]{2,0,1:T(8,128)(2,1)} %bitcast.42), calls=%async_computation | async-start | bytes 2097152 | tf_op jit(solution)/shard_map/all_to_all | solution.py:21
  15.6 0.0 copy-done.2
  15.6 0.1 copy.19
  15.7 0.1 reshape_squeeze.6
  15.8 0.1 copy.17
  15.9 0.1 broadcast_in_dim.57
  16.0 0.1 broadcast_in_dim.58
  16.1 5.0 %gather_fusion.2 = bf16[32,64,1024]{2,1,0:T(8,128)(2,1)} fusion(bf16[32,64,1024]{2,1,0:T(8,128)(2,1)} %bitcast.48, s32[1024]{0:T(1024)S(1)} %pad_clamp_fusion.1), kind=kCustom, calls=%fused_computation.2 | custom fusion | bytes 8388736 | tf_op jit(solution)/shard_map/jit(_take)/gather | solution.py:40
  21.1 3.8 %bitcast_select_fusion = bf16[8,256,1024]{2,1,0:T(8,128)(2,1)} fusion(pred[8,256]{1,0:T(8,128)(4,1)S(1)} %broadcast_in_dim.58, bf16[8,256,1024]{2,1,0:T(8,128)(2,1)} %bitcast.46), kind=kLoop, calls=%fused_computation.4 | loop fusion | flops 2097152 | bytes 8390656 | tf_op jit(solution)/shard_map/jit(_take)/select_n | solution.py:40
  24.9 0.0 copy-start.3
  24.9 6.1 %all-to-all-done = bf16[64,8,1024]{2,0,1:T(8,128)(2,1)S(1)} async-done(((bf16[64,8,1024]{2,0,1:T(8,128)(2,1)}), bf16[64,8,1024]{2,0,1:T(8,128)(2,1)S(1)}, u32[]{:S(2)}, u32[]{:S(2)}) %all-to-all-start) | async-done | bytes 1048608 | tf_op jit(solution)/shard_map/all_to_all | solution.py:21
  31.0 4.6 %all-to-all-start.1 = ((bf16[8,256,1024]{2,1,0:T(8,128)(2,1)}), bf16[8,256,1024]{2,1,0:T(8,128)(2,1)}, u32[]{:S(2)}, u32[]{:S(2)}) async-start(bf16[8,256,1024]{2,1,0:T(8,128)(2,1)} %bitcast_select_fusion), calls=%async_computation.2 | async-start | bytes 8388608 | tf_op jit(solution)/shard_map/all_to_all | solution.py:45
  35.6 0.0 reduce-scatter.3.cloned.1.call-start
  35.7 0.2 dynamic-slice_reduce_fusion
  35.8 0.0 copy-done.3
  35.8 0.1 reshape.137
  35.9 6.4 %copy.18 = bf16[1024,2048]{0,1:T(8,128)(2,1)} copy(bf16[1024,2048]{1,0:T(8,128)(2,1)} %param.9) | data formatting | bytes 8388608 | tf_op args[2]
  42.3 4.9 %gather_fusion = bf16[32,1024,64]{1,2,0:T(8,128)(2,1)} fusion(bf16[1024,32,64]{0,2,1:T(8,128)(2,1)} %bitcast.44, s32[1024]{0:T(1024)S(1)} %pad_clamp_fusion.1), kind=kCustom, calls=%fused_computation | custom fusion | bytes 8388736 | tf_op jit(solution)/shard_map/jit(_take)/gather | solution.py:19
  47.3 4.4 %fusion.4 = bf16[8,64,256]{2,1,0:T(8,128)(2,1)} fusion(bf16[1024,8,256]{0,2,1:T(8,128)(2,1)} %bitcast.45, pred[8,256]{1,0:T(8,128)(4,1)S(1)} %broadcast_in_dim.58, bf16[64,8,1024]{2,0,1:T(8,128)(2,1)S(1)} %all-to-all-done), kind=kOutput, calls=%fused_computation.10 | convolution fusion | flops 270663680 | bytes 5507072 | tf_op jit(solution)/shard_map/tri,itc->trc/dot_general | solution.py:24
  51.7 0.0 reduce-scatter.3.cloned.1.call-update
  51.7 0.0 reduce-scatter.5.cloned.1.call-start
  51.8 0.6 gather_fusion.1
  52.3 0.1 select_convert_fusion
  52.4 0.1 reshape.139
  52.5 0.0 copy-done
  52.5 0.6 constant_dynamic-slice_fusion
  53.1 0.6 iota_compare_fusion
  53.7 0.1 broadcast_in_dim.54
  53.8 0.1 broadcast_in_dim.55
  53.9 31.6 %all-to-all-done.1 = bf16[8,256,1024]{2,1,0:T(8,128)(2,1)} async-done(((bf16[8,256,1024]{2,1,0:T(8,128)(2,1)}), bf16[8,256,1024]{2,1,0:T(8,128)(2,1)}, u32[]{:S(2)}, u32[]{:S(2)}) %all-to-all-start.1) | async-done | bytes 4194336 | tf_op jit(solution)/shard_map/all_to_all | solution.py:45
  85.5 6.4 %copy.21 = bf16[8,1024,256]{2,1,0:T(8,128)(2,1)} copy(bf16[8,1024,256]{1,2,0:T(8,128)(2,1)} %bitcast.12) | data formatting | bytes 8388608 | tf_op jit(solution)/shard_map/rc,uci->rui/dot_general | solution.py:42
  91.9 0.0 reduce-scatter.3.cloned.1.call-done
  91.9 0.0 copy-start.1
  91.9 4.6 %convolution_convert_fusion = bf16[64,8192]{1,0:T(8,128)(2,1)} fusion(bf16[8192,256]{1,0:T(8,128)(2,1)} %bitcast.47, bf16[1,64,256]{2,1,0:T(8,128)(2,1)} %reduce-scatter.3.cloned.1.call-done, f32[256]{0:T(256)S(1)} %reshape.139, pred[256]{0:T(512)(128)(4,1)S(1)} %broadcast_in_dim.55), kind=kOutput, calls=%fused_computation.3 | convolution fusion | flops 269041664 | bytes 5276928 | tf_op jit(solution)/shard_map/rc,uci->rui/dot_general | solution.py:42
  96.5 0.0 reduce-scatter.5.cloned.1.call-update
  96.5 0.7 dynamic-slice_convert_fusion
  97.2 0.0 copy-done.1
  97.2 0.6 fusion.11
  97.8 25.4 %reduce-scatter.5.cloned.1.call-done = bf16[64,2048]{1,0:T(8,128)(2,1)} async-done(((bf16[64,8192]{1,0:T(8,128)(2,1)}), bf16[64,2048]{1,0:T(8,128)(2,1)}) %reduce-scatter.5.cloned.1.call-update) | async-done | bytes 262160 | tf_op jit(solution)/shard_map/reduce_scatter | solution.py:49
  123.2 1.7 %add_convert_fusion = bf16[64,2048]{1,0:T(8,128)(2,1)} fusion(bf16[64,2048]{1,0:T(8,128)(2,1)} %reduce-scatter.5.cloned.1.call-done, f32[2048]{0:T(1024)S(1)} %dynamic-slice_convert_fusion), kind=kLoop, calls=%fused_computation.13 | loop fusion | flops 393216 | bytes 532480 | tf_op jit(solution)/shard_map/convert_element_type | solution.py:54
  (6 shorter events, 0.0 us)
Async XLA Ops:
  7.2 45.3 %copy-start = (s32[8,1]{0,1:T(1,128)S(1)}, s32[8,1]{0,1:T(1,128)}, u32[]{:S(2)}) copy-start(s32[8,1]{0,1:T(1,128)} %param.13) | copy-start | bytes 100
  7.2 8.4 %copy-start.2 = (s32[8,1,4]{0,2,1:T(4,128)S(1)}, s32[8,1,4]{0,2,1:T(4,128)}, u32[]{:S(2)}) copy-start(s32[8,1,4]{0,2,1:T(4,128)} %param.12) | copy-start | bytes 388
  10.4 20.6 %all-to-all-start = ((bf16[64,8,1024]{2,0,1:T(8,128)(2,1)}), bf16[64,8,1024]{2,0,1:T(8,128)(2,1)S(1)}, u32[]{:S(2)}, u32[]{:S(2)}) async-start(bf16[64,8,1024]{2,0,1:T(8,128)(2,1)} %bitcast.42), calls=%async_computation | async-start | bytes 2097152 | tf_op jit(solution)/shard_map/all_to_all | solution.py:21
  24.9 11.0 %copy-start.3 = (bf16[2048]{0:T(1024)(128)(2,1)S(1)}, bf16[2048]{0:T(1024)(128)(2,1)}, u32[]{:S(2)}) copy-start(bf16[2048]{0:T(1024)(128)(2,1)} %param.10) | copy-start | bytes 12292
  31.0 54.4 %all-to-all-start.1 = ((bf16[8,256,1024]{2,1,0:T(8,128)(2,1)}), bf16[8,256,1024]{2,1,0:T(8,128)(2,1)}, u32[]{:S(2)}, u32[]{:S(2)}) async-start(bf16[8,256,1024]{2,1,0:T(8,128)(2,1)} %bitcast_select_fusion), calls=%async_computation.2 | async-start | bytes 8388608 | tf_op jit(solution)/shard_map/all_to_all | solution.py:45
  35.6 56.3 %reduce-scatter.3.cloned.1.call-start = ((), (), s32[]{:S(2)}) async-start(), calls=%async_computation.4 | async-start | bytes 294912 | tf_op jit(solution)/shard_map/reduce_scatter | solution.py:23
  51.7 71.5 %reduce-scatter.5.cloned.1.call-start = ((), (), s32[]{:S(2)}) async-start(), calls=%async_computation.5 | async-start | bytes 1310720 | tf_op jit(solution)/shard_map/reduce_scatter | solution.py:49
  91.9 5.3 %copy-start.1 = (bf16[1,64,256]{2,1,0:T(8,128)(2,1)S(1)}, bf16[1,64,256]{2,1,0:T(8,128)(2,1)}, u32[]{:S(2)}) copy-start(bf16[1,64,256]{2,1,0:T(8,128)(2,1)} %reduce-scatter.3.cloned.1.call-done) | copy-start | bytes 98308
Sparse Core Ops, SparseCore 0:
  51.8 35.4 reduce-scatter.2
  96.6 26.5 reduce-scatter.4
where the time goes:
time: 133 us; the launch traced here: 132 us
  waiting for transfers between devices  63.1 us (47%)
  local copies, waits for them, and re-layouts  26 us (20%)
  between operations  14.1 us (11%)
  starting transfers between devices  9.82 us (7%)
  other arithmetic  9.73 us (7%)
  matrix products  8.96 us (7%)
    all_to_all x1, waiting for transfers between devices, on_device(): lax.all_to_all(outgoing, 'tok', split_axis=0, concat_axis=0, tiled=True)  31.6 us
    reduce_scatter x1, waiting for transfers between devices, on_device(): lax.psum_scatter(owner_part.astype(jnp.bfloat16), 'feat', scatter_dimensi...  25.4 us
    unnamed x10, local copies, waits for them, and re-layouts  6.51 us
    dot_general x1, local copies, waits for them, and re-layouts, on_device(): jnp.einsum('rc,uci->rui', code_values, lax.all_to_all(outgoing, 'tok', sp...  6.44 us
    all_to_all x1, waiting for transfers between devices, on_device(): lax.all_to_all(centered, 'tok', split_axis=1, concat_axis=0, tiled=True)  6.14 us
    all_to_all x1, starting transfers between devices, on_device(): lax.all_to_all(centered, 'tok', split_axis=1, concat_axis=0, tiled=True)  5.17 us
    gather x1, local copies, waits for them, and re-layouts, on_device(): jnp.take(dec_weight.reshape(nblocks, BLOCK, wslice), listed, axis=0)  4.98 us
    gather x1, local copies, waits for them, and re-layouts, on_device(): jnp.take(enc_weight.reshape(wslice, nblocks, BLOCK), listed, axis=1)  4.95 us
  transfers between devices with their start and end apart: 4, of which 3 were waited for; matrix products, arithmetic and copies ran while one was open for 27% of the time, Pallas kernels for 0%

commit v1 on v0

--- a/solution.py
+++ b/solution.py
@@ -18,7 +18,10 @@
     centered = (tokens.astype(jnp.float32) - dec_bias.astype(jnp.float32)).astype(jnp.bfloat16)
     chosen = jnp.take(enc_weight.reshape(wslice, nblocks, BLOCK), listed, axis=1)
     chosen = chosen.reshape(wslice, tile_count, active_cols)
-    gathered = lax.all_to_all(centered, "tok", split_axis=1, concat_axis=0, tiled=True)
+    gathered = jnp.concatenate(
+        lax.all_to_all(jnp.stack(jnp.split(centered, lax.axis_size("tok"), axis=1)), "tok", 0, 0),
+        axis=0,
+    )
     gathered = gathered.reshape(tile_count, tok_rows, wslice)
     pre = lax.psum_scatter(
         jnp.einsum("tri,itc->trc", gathered, chosen, preferred_element_type=jnp.float32).astype(

time: 133 us -> 137 us (1.030)
  local copies, waits for them, and re-layouts: 26 us -> 30.2 us
    unnamed x10 -> x17, local copies, waits for them, and re-layouts: 6.51 us -> 11.2 us
  transfers between devices with their start and end apart: 4 -> 4, of which waited for: 3 -> 3; matrix products, arithmetic and copies ran while one was open for 27% -> 26% of each run, Pallas kernels for 0% -> 0%
where the time goes in v1:
time: 137 us; the launch traced here: 136 us
  waiting for transfers between devices  63.1 us (46%)
  local copies, waits for them, and re-layouts  30.2 us (22%)
  between operations  14.1 us (10%)
  starting transfers between devices  9.81 us (7%)
  other arithmetic  9.73 us (7%)
  matrix products  8.96 us (7%)
    all_to_all x1, waiting for transfers between devices, on_device(): lax.all_to_all(outgoing, 'tok', split_axis=0, concat_axis=0, tiled=True)  31.8 us
    reduce_scatter x1, waiting for transfers between devices, on_device(): lax.psum_scatter(owner_part.astype(jnp.bfloat16), 'feat', scatter_dimensi...  25.3 us
    unnamed x17, local copies, waits for them, and re-layouts  11.2 us
    dot_general x1, local copies, waits for them, and re-layouts, on_device(): jnp.einsum('rc,uci->rui', code_values, lax.all_to_all(outgoing, 'tok', sp...  6.43 us
    all_to_all x1, waiting for transfers between devices, on_device(): lax.all_to_all(jnp.stack(jnp.split(centered, lax.axis_size('tok'), axis=1...  5.95 us
    all_to_all x1, starting transfers between devices, on_device(): lax.all_to_all(jnp.stack(jnp.split(centered, lax.axis_size('tok'), axis=1...  5.17 us
    gather x1, local copies, waits for them, and re-layouts, on_device(): jnp.take(dec_weight.reshape(nblocks, BLOCK, wslice), listed, axis=0)  4.98 us
    gather x1, local copies, waits for them, and re-layouts, on_device(): jnp.take(enc_weight.reshape(wslice, nblocks, BLOCK), listed, axis=1)  4.94 us
  transfers between devices with their start and end apart: 4, of which 3 were waited for; matrix products, arithmetic and copies ran while one was open for 26% of the time, Pallas kernels for 0%

profile of v1, /device:TPU:0, one launch (start us, length us, event | category | flops | bytes accessed | tf_op | source)
XLA Modules:
  0.0 135.9 jit_solution(1448392874445939644)
XLA Ops:
  7.2 0.0 copy-start
  7.2 0.0 copy-start.2
  7.2 0.7 convert_element_type.46
  7.9 1.4 %subtract_convert_fusion = bf16[64,8192]{1,0:T(8,128)(2,1)S(1)} fusion(bf16[64,8192]{1,0:T(8,128)(2,1)} %param.7, f32[8192]{0:T(1024)S(1)} %convert_element_type.46), kind=kLoop, calls=%fused_computation.9 | loop fusion | flops 1572864 | bytes 2129920 | tf_op jit(solution)/shard_map/convert_element_type | solution.py:18
  9.3 0.7 fusion.14
  10.0 0.7 fusion.13
  10.6 0.7 fusion.12
  11.3 0.7 fusion.11
  12.0 0.7 fusion.10
  12.6 0.7 fusion.9
  13.3 0.7 fusion.8
  14.0 0.7 fusion.7
  14.6 5.2 %all-to-all-start = ((bf16[8,64,1024]{2,1,0:T(8,128)(2,1)}), bf16[8,64,1024]{2,1,0:T(8,128)(2,1)S(1)}, u32[]{:S(2)}, u32[]{:S(2)}) async-start(bf16[8,64,1024]{2,1,0:T(8,128)(2,1)} %fusion.7), calls=%async_computation | async-start | bytes 2097152 | tf_op jit(solution)/shard_map/all_to_all | solution.py:22
  19.8 0.0 copy-done.2
  19.8 0.1 copy.17
  19.9 0.2 dynamic-slice_reduce_fusion
  20.1 0.1 reshape_squeeze.6
  20.2 0.1 copy.15
  20.3 0.1 broadcast_in_dim.57
  20.4 0.1 broadcast_in_dim.58
  20.5 5.0 %gather_fusion.2 = bf16[32,64,1024]{2,1,0:T(8,128)(2,1)} fusion(bf16[32,64,1024]{2,1,0:T(8,128)(2,1)} %bitcast.74, s32[1024]{0:T(1024)S(1)} %get-tuple-element.3), kind=kCustom, calls=%fused_computation.2 | custom fusion | bytes 8388736 | tf_op jit(solution)/shard_map/jit(_take)/gather | solution.py:43
  25.5 3.8 %bitcast_select_fusion = bf16[8,256,1024]{2,1,0:T(8,128)(2,1)} fusion(pred[8,256]{1,0:T(8,128)(4,1)S(1)} %broadcast_in_dim.58, bf16[8,256,1024]{2,1,0:T(8,128)(2,1)} %bitcast.72), kind=kLoop, calls=%fused_computation.4 | loop fusion | flops 2097152 | bytes 8390656 | tf_op jit(solution)/shard_map/jit(_take)/select_n | solution.py:43
  29.3 6.0 %all-to-all-done = bf16[8,64,1024]{2,1,0:T(8,128)(2,1)S(1)} async-done(((bf16[8,64,1024]{2,1,0:T(8,128)(2,1)}), bf16[8,64,1024]{2,1,0:T(8,128)(2,1)S(1)}, u32[]{:S(2)}, u32[]{:S(2)}) %all-to-all-start) | async-done | bytes 1048608 | tf_op jit(solution)/shard_map/all_to_all | solution.py:22
  35.2 4.6 %all-to-all-start.1 = ((bf16[8,256,1024]{2,1,0:T(8,128)(2,1)}), bf16[8,256,1024]{2,1,0:T(8,128)(2,1)}, u32[]{:S(2)}, u32[]{:S(2)}) async-start(bf16[8,256,1024]{2,1,0:T(8,128)(2,1)} %bitcast_select_fusion), calls=%async_computation.2 | async-start | bytes 8388608 | tf_op jit(solution)/shard_map/all_to_all | solution.py:48
  39.8 0.0 reduce-scatter.3.cloned.1.call-start
  39.8 6.4 %copy.16 = bf16[1024,2048]{0,1:T(8,128)(2,1)} copy(bf16[1024,2048]{1,0:T(8,128)(2,1)} %param.9) | data formatting | bytes 8388608 | tf_op args[2]
  46.2 4.9 %gather_fusion = bf16[32,1024,64]{1,2,0:T(8,128)(2,1)} fusion(bf16[1024,32,64]{0,2,1:T(8,128)(2,1)} %bitcast.70, s32[1024]{0:T(1024)S(1)} %get-tuple-element.3), kind=kCustom, calls=%fused_computation | custom fusion | bytes 8388736 | tf_op jit(solution)/shard_map/jit(_take)/gather | solution.py:19
  51.2 0.0 copy-start.3
  51.2 4.4 %fusion.4 = bf16[8,64,256]{2,1,0:T(8,128)(2,1)} fusion(bf16[8,64,1024]{2,1,0:T(8,128)(2,1)S(1)} %all-to-all-done, bf16[1024,8,256]{0,2,1:T(8,128)(2,1)} %bitcast.71, pred[8,256]{1,0:T(8,128)(4,1)S(1)} %broadcast_in_dim.58), kind=kOutput, calls=%fused_computation.10 | convolution fusion | flops 270663680 | bytes 5507072 | tf_op jit(solution)/shard_map/tri,itc->trc/dot_general | solution.py:27
  55.6 0.0 reduce-scatter.3.cloned.1.call-update
  55.6 0.0 reduce-scatter.5.cloned.1.call-start
  55.7 0.0 copy-done.3
  55.7 0.1 reshape.132
  55.8 0.6 gather_fusion.1
  56.3 0.1 select_convert_fusion
  56.4 0.1 reshape.134
  56.5 0.0 copy-done
  56.5 0.6 constant_dynamic-slice_fusion
  57.1 0.6 iota_compare_fusion
  57.7 0.1 broadcast_in_dim.54
  57.8 0.1 broadcast_in_dim.55
  57.9 31.8 %all-to-all-done.1 = bf16[8,256,1024]{2,1,0:T(8,128)(2,1)} async-done(((bf16[8,256,1024]{2,1,0:T(8,128)(2,1)}), bf16[8,256,1024]{2,1,0:T(8,128)(2,1)}, u32[]{:S(2)}, u32[]{:S(2)}) %all-to-all-start.1) | async-done | bytes 4194336 | tf_op jit(solution)/shard_map/all_to_all | solution.py:48
  89.7 6.4 %copy.19 = bf16[8,1024,256]{2,1,0:T(8,128)(2,1)} copy(bf16[8,1024,256]{1,2,0:T(8,128)(2,1)} %bitcast.19) | data formatting | bytes 8388608 | tf_op jit(solution)/shard_map/rc,uci->rui/dot_general | solution.py:45
  96.1 0.0 reduce-scatter.3.cloned.1.call-done
  96.1 0.0 copy-start.1
  96.1 4.6 %convolution_convert_fusion = bf16[64,8192]{1,0:T(8,128)(2,1)} fusion(bf16[8192,256]{1,0:T(8,128)(2,1)} %bitcast.73, bf16[1,64,256]{2,1,0:T(8,128)(2,1)} %reduce-scatter.3.cloned.1.call-done, f32[256]{0:T(256)S(1)} %reshape.134, pred[256]{0:T(512)(128)(4,1)S(1)} %broadcast_in_dim.55), kind=kOutput, calls=%fused_computation.3 | convolution fusion | flops 269041664 | bytes 5276928 | tf_op jit(solution)/shard_map/rc,uci->rui/dot_general | solution.py:45
  100.7 0.0 reduce-scatter.5.cloned.1.call-update
  100.7 0.7 dynamic-slice_convert_fusion
  101.4 0.0 copy-done.1
  101.4 0.6 fusion.18
  102.0 25.3 %reduce-scatter.5.cloned.1.call-done = bf16[64,2048]{1,0:T(8,128)(2,1)} async-done(((bf16[64,8192]{1,0:T(8,128)(2,1)}), bf16[64,2048]{1,0:T(8,128)(2,1)}) %reduce-scatter.5.cloned.1.call-update) | async-done | bytes 262160 | tf_op jit(solution)/shard_map/reduce_scatter | solution.py:52
  127.4 1.7 %add_convert_fusion = bf16[64,2048]{1,0:T(8,128)(2,1)} fusion(bf16[64,2048]{1,0:T(8,128)(2,1)} %reduce-scatter.5.cloned.1.call-done, f32[2048]{0:T(1024)S(1)} %dynamic-slice_convert_fusion), kind=kLoop, calls=%fused_computation.11 | loop fusion | flops 393216 | bytes 532480 | tf_op jit(solution)/shard_map/convert_element_type | solution.py:57
  (5 shorter events, 0.0 us)
Async XLA Ops:
  7.2 49.3 %copy-start = (s32[8,1]{0,1:T(1,128)S(1)}, s32[8,1]{0,1:T(1,128)}, u32[]{:S(2)}) copy-start(s32[8,1]{0,1:T(1,128)} %param.13) | copy-start | bytes 100
  7.2 12.6 %copy-start.2 = (s32[8,1,4]{0,2,1:T(4,128)S(1)}, s32[8,1,4]{0,2,1:T(4,128)}, u32[]{:S(2)}) copy-start(s32[8,1,4]{0,2,1:T(4,128)} %param.12) | copy-start | bytes 388
  14.6 20.6 %all-to-all-start = ((bf16[8,64,1024]{2,1,0:T(8,128)(2,1)}), bf16[8,64,1024]{2,1,0:T(8,128)(2,1)S(1)}, u32[]{:S(2)}, u32[]{:S(2)}) async-start(bf16[8,64,1024]{2,1,0:T(8,128)(2,1)} %fusion.7), calls=%async_computation | async-start | bytes 2097152 | tf_op jit(solution)/shard_map/all_to_all | solution.py:22
  35.2 54.5 %all-to-all-start.1 = ((bf16[8,256,1024]{2,1,0:T(8,128)(2,1)}), bf16[8,256,1024]{2,1,0:T(8,128)(2,1)}, u32[]{:S(2)}, u32[]{:S(2)}) async-start(bf16[8,256,1024]{2,1,0:T(8,128)(2,1)} %bitcast_select_fusion), calls=%async_computation.2 | async-start | bytes 8388608 | tf_op jit(solution)/shard_map/all_to_all | solution.py:48
  39.8 56.3 %reduce-scatter.3.cloned.1.call-start = ((), (), s32[]{:S(2)}) async-start(), calls=%async_computation.4 | async-start | bytes 294912 | tf_op jit(solution)/shard_map/reduce_scatter | solution.py:26
  51.2 4.5 %copy-start.3 = (bf16[2048]{0:T(1024)(128)(2,1)S(1)}, bf16[2048]{0:T(1024)(128)(2,1)}, u32[]{:S(2)}) copy-start(bf16[2048]{0:T(1024)(128)(2,1)} %param.10) | copy-start | bytes 12292
  55.6 71.8 %reduce-scatter.5.cloned.1.call-start = ((), (), s32[]{:S(2)}) async-start(), calls=%async_computation.5 | async-start | bytes 1310720 | tf_op jit(solution)/shard_map/reduce_scatter | solution.py:52
  96.1 5.3 %copy-start.1 = (bf16[1,64,256]{2,1,0:T(8,128)(2,1)S(1)}, bf16[1,64,256]{2,1,0:T(8,128)(2,1)}, u32[]{:S(2)}) copy-start(bf16[1,64,256]{2,1,0:T(8,128)(2,1)} %reduce-scatter.3.cloned.1.call-done) | copy-start | bytes 98308
Sparse Core Ops, SparseCore 0:
  55.7 35.5 reduce-scatter.2
  100.8 26.5 reduce-scatter.4
